TPU v7x, 32 devices: a whole 2x2x4 slice. The times are simulated.
32 devices in a mesh: pipe: 2 (over core), row: 4 (over z), rep: 4 (over y, x).
Axes of the slice: x: 2, y: 2, z: 4, core: 2. Of those that a mesh axis runs over, the one named last changes fastest.
Arguments:
- features: bfloat16 [1, 4096, 256], P(None, ('pipe', 'row')), may hold values from -6 to 6
- tile_src: int32 [8, 4, 2, 12], P(('pipe', 'row'), 'rep'), may hold values from 0 to 7
- tile_dst: int32 [8, 4, 2, 12], P(('pipe', 'row'), 'rep'), may hold values from 0 to 7
- tile_count: int32 [8, 4, 2], P(('pipe', 'row'), 'rep'), may hold values from 1 to 12, as said below
- edge_dst: int32 [8, 4, 2, 12, 256], P(('pipe', 'row'), 'rep'), may hold values from 0 to 63
- edge_src: int32 [8, 4, 2, 12, 256], P(('pipe', 'row'), 'rep'), may hold values from 0 to 63
- edge_weight: float32 [8, 4, 2, 12, 256], P(('pipe', 'row'), 'rep'), may hold values from 0.25 to 4
- w_msg: bfloat16 [2, 256, 256], replicated, may hold values from -0.375 to 0.375
- w_self: bfloat16 [2, 256, 256], replicated, may hold values from -0.375 to 0.375
- w_mid: bfloat16 [2, 256, 256], replicated, may hold values from -0.375 to 0.375
- w_out: bfloat16 [2, 256, 256], replicated, may hold values from -0.375 to 0.375
- gain: float32 [2, 256], replicated, may hold values from 0.1 to 1.9
Outputs:
- hidden: bfloat16 [2, 1, 4096, 256], P(None, None, ('pipe', 'row'))
Inputs may be any that keep to these rules, and one draw needn't show every extreme that they name: `tile_count`: every entry is at least 1 and at most 12; for every row block and every index of rep, some section has exactly 12 live slots.
All inputs are finite; a program needn't handle non-finite values.
Results may differ from a plain program's by a relative error of at most 0.0054.
Values may be sent and summed in bfloat16 or wider, within the bound.
A program may use at most 64 MiB of HBM per device.

v0:
```python
import jax
import jax.numpy as jnp
from jax import lax
from jax.sharding import PartitionSpec as P

BS = 64
LAYERS = 2


def build_tiles(dst, src, weight):
    hot_dst = (dst[..., None] == jnp.arange(BS)).astype(jnp.float32) * weight[..., None]
    hot_src = (src[..., None] == jnp.arange(BS)).astype(jnp.float32)
    made = jnp.einsum("...ea,...eb->...ab", hot_dst, hot_src, precision=lax.Precision.HIGHEST)
    return made.astype(jnp.bfloat16)


def section_product(source, tiles_now, src_now, hot_now):
    rows, width = source.shape
    blocked = source.reshape(rows // BS, BS, width)
    picked = jnp.take(blocked, src_now, axis=0)
    prod = jnp.einsum("kab,kbf->kaf", tiles_now, picked, preferred_element_type=jnp.float32)
    summed = jnp.einsum("kn,kaf->naf", hot_now, prod, precision=lax.Precision.HIGHEST)
    return summed.reshape(rows, width)


def update_rows(rows_in, summed, wself, wmid, wout, gain_row):
    stat = jnp.mean(summed * summed, axis=-1, keepdims=True)
    normed = summed * lax.rsqrt(stat + 1e-05) * gain_row
    pre = jnp.dot(rows_in, wself, preferred_element_type=jnp.float32) + normed
    first = jax.nn.silu(pre).astype(jnp.bfloat16)
    second = jax.nn.silu(jnp.dot(first, wmid, preferred_element_type=jnp.float32)).astype(
        jnp.bfloat16
    )
    return (
        rows_in.astype(jnp.float32) + jnp.dot(second, wout, preferred_element_type=jnp.float32)
    ).astype(jnp.bfloat16)


def on_device(
    features,
    tile_src,
    tile_dst,
    tile_count,
    edge_dst,
    edge_src,
    edge_weight,
    w_msg,
    w_self,
    w_mid,
    w_out,
    gain,
):
    events, rows, width = features.shape
    blocks = rows // BS
    slots = tile_src.shape[3]
    rep_count = lax.axis_size("rep")
    my_rep = lax.axis_index("rep")
    quarter = width // rep_count
    tiles = build_tiles(edge_dst[0, 0], edge_src[0, 0], edge_weight[0, 0])
    live_int = (jnp.arange(slots)[None, :] < tile_count[0, 0][:, None]).astype(jnp.int32)
    src_idx = tile_src[0, 0]
    dst_idx = tile_dst[0, 0]
    tiles_all = lax.all_gather(tiles[None], "rep", axis=0, tiled=True)
    index_all = lax.all_gather(
        jnp.stack([src_idx, dst_idx, live_int])[None], "rep", axis=0, tiled=True
    )
    results = []
    for level in range(LAYERS):
        results.append([])
    state = features[0]
    for level in range(LAYERS):
        wmsg = w_msg[level]
        wself = w_self[level]
        wmid = w_mid[level]
        wout = w_out[level]
        gain_row = gain[level]
        y = jnp.dot(state, wmsg, preferred_element_type=jnp.float32).astype(jnp.bfloat16)
        y_share = lax.dynamic_slice_in_dim(y, my_rep * quarter, quarter, 1)
        piece = lax.all_gather(y_share, ("pipe", "row"), axis=0, tiled=True)
        count = piece.shape[0] // rows

        def one_block(i, acc):
            owner_rep = i % rep_count
            section = i // rep_count
            tiles_rep = lax.dynamic_index_in_dim(tiles_all, owner_rep, 0, keepdims=False)
            tiles_now = lax.dynamic_index_in_dim(tiles_rep, section, 0, keepdims=False)
            info_rep = lax.dynamic_index_in_dim(index_all, owner_rep, 0, keepdims=False)
            info = lax.dynamic_index_in_dim(info_rep, section, 1, keepdims=False)
            hot_now = (info[1][:, None] == jnp.arange(blocks)).astype(jnp.float32) * info[2].astype(
                jnp.float32
            )[:, None]
            sub = lax.dynamic_slice_in_dim(piece, i * rows, rows, 0)
            return acc + section_product(sub, tiles_now, info[0], hot_now)

        column_sum = lax.fori_loop(0, count, one_block, jnp.zeros((rows, quarter), jnp.float32))
        summed = lax.all_gather(column_sum, "rep", axis=1, tiled=True)
        state = update_rows(state, summed, wself, wmid, wout, gain_row)
        results[level].append(state)
    return jnp.stack([jnp.stack(items) for items in results])


def solution(mesh):
    placed = (
        P(None, ("pipe", "row"), None),
        P(("pipe", "row"), "rep", None, None),
        P(("pipe", "row"), "rep", None, None),
        P(("pipe", "row"), "rep", None),
        P(("pipe", "row"), "rep", None, None, None),
        P(("pipe", "row"), "rep", None, None, None),
        P(("pipe", "row"), "rep", None, None, None),
        P(),
        P(),
        P(),
        P(),
        P(),
    )
    return jax.shard_map(
        on_device,
        mesh=mesh,
        in_specs=placed,
        out_specs=P(None, None, ("pipe", "row"), None),
        check_vma=False,
    )
```

profile of v0, /device:TPU:0, one launch (start us, length us, event | category | flops | bytes accessed | tf_op | source)
XLA Modules:
  0.0 140.6 jit_solution(12819187617356729768)
XLA Ops:
  0.0 1.2 fusion.56
  1.3 27.9 %all_gather.20 = bf16[4096,64]{0,1:T(8,128)(2,1)S(1)} all-gather(bf16[512,64]{0,1:T(8,128)(2,1)S(1)} %dynamic-slice_convert_fusion.1), channel_id=1, replica_groups=mesh['pipe'=2,'row'=4,'rep'=4] {'pipe','row'}, dimensions={0}, use_global_device_ids=true | all-gather | bytes 589824 | tf_op jit(solution)/shard_map/all_gather | solution.py:79
  29.2 0.7 copy.31
  29.9 0.7 copy.32
  30.6 0.7 copy.33
  31.4 1.2 fusion.40
  32.6 18.9 %all-gather.1 = bf16[8,12,64,64]{3,2,1,0:T(8,128)(2,1)S(1)} all-gather(bf16[2,12,64,64]{3,2,1,0:T(8,128)(2,1)S(1)} %fusion.40), channel_id=3, replica_groups=mesh['pipe'=2,'row'=4,'rep'=4] {'rep'}, dimensions={0}, use_global_device_ids=true | all-gather | bytes 983040 | tf_op jit(solution)/shard_map/all_gather | solution.py:63
  51.6 8.3 %all-gather = s32[12,2,12]{2,1,0:T(2,128)S(1)} all-gather(s32[3,2,12]{2,1,0:T(2,128)S(1)} %pad_add_fusion), channel_id=2, replica_groups=mesh['pipe'=2,'row'=4,'rep'=4] {'rep'}, dimensions={0}, use_global_device_ids=true | all-gather | bytes 1440 | tf_op jit(solution)/shard_map/all_gather | solution.py:64
  59.9 15.6 %while.34 = (s32[]{:T(128)}, f32[512,64]{0,1:T(8,128)S(1)}, s32[4,3,2,12]{3,2,1,0:T(2,128)S(1)}, bf16[4,2,12,64,64]{4,3,2,1,0:T(8,128)(2,1)S(1)}, bf16[4096,64]{...) while((s32[]{:T(128)}, f32[512,64]{0,1:T(8,128)S(1)}, ...), condition=%wide.region_1.3_spmd.clone, body=%wide.region_0.2_spmd.clone.sunk | while | flops 11126065 | bytes 2430404 | solution.py:95
  60.1 0.6 gather_fusion
  62.1 0.6 gather_fusion
  64.0 0.6 gather_fusion
  66.0 0.6 gather_fusion
  67.9 0.6 gather_fusion
  69.9 0.6 gather_fusion
  71.8 0.6 gather_fusion
  73.8 0.6 gather_fusion
  75.6 9.3 %all_gather.21 = f32[512,256]{0,1:T(8,128)S(1)} all-gather(f32[512,64]{0,1:T(8,128)S(1)} %get-tuple-element.330), channel_id=1, replica_groups=mesh['pipe'=2,'row'=4,'rep'=4] {'rep'}, dimensions={1}, use_global_device_ids=true | all-gather | bytes 655360 | tf_op jit(solution)/shard_map/all_gather | solution.py:96
  85.2 1.4 multiply_convert_fusion.2
  87.2 26.4 %all_gather.22 = bf16[4096,64]{0,1:T(8,128)(2,1)S(1)} all-gather(bf16[512,64]{0,1:T(8,128)(2,1)S(1)} %dynamic-slice_convert_fusion), channel_id=1, replica_groups=mesh['pipe'=2,'row'=4,'rep'=4] {'pipe','row'}, dimensions={0}, use_global_device_ids=true | all-gather | bytes 589824 | tf_op jit(solution)/shard_map/all_gather | solution.py:79
  113.6 15.5 %while.35 = (s32[]{:T(128)}, f32[512,64]{0,1:T(8,128)S(1)}, s32[4,3,2,12]{3,2,1,0:T(2,128)S(1)}, bf16[4,2,12,64,64]{4,3,2,1,0:T(8,128)(2,1)S(1)}, bf16[4096,64]{...) while((s32[]{:T(128)}, f32[512,64]{0,1:T(8,128)S(1)}, ...), condition=%wide.region_4.6_spmd.clone, body=%wide.region_3.5_spmd.clone.sunk | while | flops 11126065 | bytes 2430404 | solution.py:95
  113.8 0.6 gather_fusion.1
  129.2 9.1 %all_gather.23 = f32[512,256]{0,1:T(8,128)S(1)} all-gather(f32[512,64]{0,1:T(8,128)S(1)} %get-tuple-element.331), channel_id=1, replica_groups=mesh['pipe'=2,'row'=4,'rep'=4] {'rep'}, dimensions={1}, use_global_device_ids=true | all-gather | bytes 655360 | tf_op jit(solution)/shard_map/all_gather | solution.py:96
  139.8 0.8 pad_maximum_fusion
  (206 shorter events, 26.4 us)
Async XLA Ops:
  31.4 20.1 %copy-start.10 = (s32[1,1,2]{2,1,0:T(1,128)S(1)}, s32[1,1,2]{2,1,0:T(1,128)}, u32[]{:S(2)}) copy-start(s32[1,1,2]{2,1,0:T(1,128)} %param.21) | copy-start | bytes 28
  31.4 20.2 %copy-start.5 = (s32[1,1,2,12]{3,2,1,0:T(2,128)S(1)}, s32[1,1,2,12]{3,2,1,0:T(2,128)}, u32[]{:S(2)}) copy-start(s32[1,1,2,12]{3,2,1,0:T(2,128)} %param.20) | copy-start | bytes 292
  31.4 20.2 %copy-start.6 = (s32[1,1,2,12]{3,2,1,0:T(2,128)S(1)}, s32[1,1,2,12]{3,2,1,0:T(2,128)}, u32[]{:S(2)}) copy-start(s32[1,1,2,12]{3,2,1,0:T(2,128)} %param.19) | copy-start | bytes 292
  75.5 9.6 %copy-start.4 = (f32[2,256]{1,0:T(2,128)S(1)}, f32[2,256]{1,0:T(2,128)}, u32[]{:S(2)}) copy-start(f32[2,256]{1,0:T(2,128)} %param.29) | copy-start | bytes 6148
  75.5 9.6 %copy-start = (bf16[1,512,256]{2,1,0:T(8,128)(2,1)S(1)}, bf16[1,512,256]{2,1,0:T(8,128)(2,1)}, u32[]{:S(2)}) copy-start(bf16[1,512,256]{2,1,0:T(8,128)(2,1)} %param.18) | copy-start | bytes 786436
  75.6 9.6 %copy-start.7 = (bf16[2,256,256]{2,1,0:T(8,128)(2,1)S(1)}, bf16[2,256,256]{2,1,0:T(8,128)(2,1)}, u32[]{:S(2)}) copy-start(bf16[2,256,256]{2,1,0:T(8,128)(2,1)} %param.27) | copy-start | bytes 786436
  85.2 1.4 %copy-start.2 = (bf16[2,256,256]{2,1,0:T(8,128)(2,1)S(1)}, bf16[2,256,256]{2,1,0:T(8,128)(2,1)}, u32[]{:S(2)}) copy-start(bf16[2,256,256]{2,1,0:T(8,128)(2,1)} %param.28) | copy-start | bytes 786436
  85.2 1.7 %copy-start.1 = (bf16[2,256,256]{2,1,0:T(8,128)(2,1)S(1)}, bf16[2,256,256]{2,1,0:T(8,128)(2,1)}, u32[]{:S(2)}) copy-start(bf16[2,256,256]{2,1,0:T(8,128)(2,1)} %param.25) | copy-start | bytes 786436
  129.1 9.4 %copy-start.8 = (bf16[2,256,256]{2,1,0:T(8,128)(2,1)S(1)}, bf16[2,256,256]{2,1,0:T(8,128)(2,1)}, u32[]{:S(2)}) copy-start(bf16[2,256,256]{2,1,0:T(8,128)(2,1)} %param.27) | copy-start | bytes 786436
  129.1 9.4 %copy-start.9 = (bf16[2,256,256]{2,1,0:T(8,128)(2,1)S(1)}, bf16[2,256,256]{2,1,0:T(8,128)(2,1)}, u32[]{:S(2)}) copy-start(bf16[2,256,256]{2,1,0:T(8,128)(2,1)} %param.26) | copy-start | bytes 786436
  138.6 1.0 copy-start.3
where the time goes:
time: 141 us
  blocking collectives  100 us (71%)
  local copies, waits for them, and re-layouts  20.9 us (15%)
  matrix products  15.4 us (11%)
  other arithmetic  2.33 us (2%)
  loops' own time  1.8 us (1%)
    all_gather x2, blocking collectives, on_device(): piece = lax.all_gather(y_share, ('pipe', 'row'), axis=0, tiled=True)  54.3 us
    all_gather x1, blocking collectives, on_device(): tiles_all = lax.all_gather(tiles[None], 'rep', axis=0, tiled=True)  18.9 us
    all_gather x2, blocking collectives, on_device(): summed = lax.all_gather(column_sum, 'rep', axis=1, tiled=True)  18.4 us
    gather x16, local copies, waits for them, and re-layouts, section_product(): picked = jnp.take(blocked, src_now, axis=0)  9.42 us
    all_gather x1, blocking collectives, on_device(): lax.all_gather(jnp.stack([src_idx, dst_idx, live_int])[None], 'rep', axis...  8.33 us
    dot_general x16, matrix products, section_product(): jnp.einsum('kn,kaf->naf', hot_now, prod, precision=lax.Precision.HIGHEST)  6.06 us
    dot_general x16, local copies, waits for them, and re-layouts, section_product(): jnp.einsum('kab,kbf->kaf', tiles_now, picked, preferred_element_type=jnp....  4.37 us
    dot_general x16, matrix products, section_product(): jnp.einsum('kab,kbf->kaf', tiles_now, picked, preferred_element_type=jnp....  4.28 us

commit v1 on v0

--- a/solution.py
+++ b/solution.py
@@ -1,10 +1,17 @@
+import functools
+
 import jax
 import jax.numpy as jnp
 from jax import lax
+from jax.experimental import pallas as pl
+from jax.experimental.pallas import tpu as pltpu
 from jax.sharding import PartitionSpec as P
 
 BS = 64
 LAYERS = 2
+LANES = 128
+HALF = 64
+MESH = pl.DeviceIdType.MESH
 
 
 def build_tiles(dst, src, weight):
@@ -36,7 +43,7 @@
     ).astype(jnp.bfloat16)
 
 
-def on_device(
+def by_sections(
     features,
     tile_src,
     tile_dst,
@@ -99,6 +106,257 @@
     return jnp.stack([jnp.stack(items) for items in results])
 
 
+def fused_body(sizes, x_ref, code_ref, edst_ref, esrc_ref, ew_ref, wmsg_ref, wself_ref, wmid_ref, wout_ref, gain_ref,
+               out_ref, code_v, code_s, edst_v, esrc_v, ew_v, big, ybuf, cbuf, pick0, pick1,
+               e_send, e_recv, l_sem, y_send, y_recv, f_send, f_recv, c_send, c_recv):
+    rows, width, slots, sections, rep_n, row_n = sizes
+    half_rows = rows // 2
+    per_half = half_rows // BS
+    rep, row, pipe = lax.axis_index("rep"), lax.axis_index("row"), lax.axis_index("pipe")
+    other = 1 - pipe
+
+    def at_rep(o):
+        return lax.rem(rep + o, rep_n)
+
+    def at_row(o):
+        return lax.rem(row + o, row_n)
+
+    barrier = pltpu.get_barrier_semaphore()
+    for o in range(1, rep_n):
+        pl.semaphore_signal(barrier, inc=1, device_id={"rep": at_rep(o)}, device_id_type=MESH)
+    for o in range(1, row_n):
+        pl.semaphore_signal(barrier, inc=1, device_id={"row": at_row(o)}, device_id_type=MESH)
+    pl.semaphore_signal(barrier, inc=1, device_id={"pipe": other}, device_id_type=MESH)
+
+    lane = lax.broadcasted_iota(jnp.int32, (1, LANES), 1)
+    low = lane < HALF
+
+    def project(level, state):
+        w = wmsg_ref[level]
+        lo = jnp.zeros((width, LANES), jnp.bfloat16)
+        hi = lo
+        for r in range(rep_n):
+            base = (r // 2) * LANES
+            w128 = w[:, base:base + LANES]
+            rolled = jnp.concatenate([w128[:, HALF:], w128[:, :HALF]], axis=1)
+            first, second = (w128, rolled) if r % 2 == 0 else (rolled, w128)
+            pick = (rep == r).astype(jnp.float32)
+            lo = lo + first * (jnp.where(low, 1.0, 0.0) * pick).astype(jnp.bfloat16)
+            hi = hi + second * (jnp.where(low, 0.0, 1.0) * pick).astype(jnp.bfloat16)
+        packed = jnp.dot(state[:half_rows], lo, preferred_element_type=jnp.float32)
+        packed = packed + jnp.dot(state[half_rows:], hi, preferred_element_type=jnp.float32)
+        ybuf[level, pipe * row_n + row] = packed.astype(jnp.bfloat16).reshape(per_half, BS, LANES)
+
+    def y_copy(level, o):
+        mine = ybuf.at[level, pipe * row_n + row]
+        return pltpu.make_async_remote_copy(mine, mine, y_send.at[level, o], y_recv.at[level, o],
+                                            device_id={"row": at_row(o)}, device_id_type=MESH)
+
+    def forward(level, o):
+        block = ybuf.at[level, pipe * row_n + at_row(row_n - o)]
+        return pltpu.make_async_remote_copy(block, block, f_send.at[level, o], f_recv.at[level, o],
+                                            device_id={"pipe": other}, device_id_type=MESH)
+
+    def edge_copies(o):
+        made = []
+        for i, (src, dst) in enumerate(((code_ref, code_v), (edst_ref, edst_v), (esrc_ref, esrc_v), (ew_ref, ew_v))):
+            made.append(pltpu.make_async_remote_copy(src, dst.at[rep], e_send.at[o, i], e_recv.at[o, i],
+                                                     device_id={"rep": at_rep(o)}, device_id_type=MESH))
+        return made
+
+    local = [pltpu.make_async_copy(src, dst.at[rep], l_sem.at[i]) for i, (src, dst) in enumerate(
+        ((code_ref, code_s), (edst_ref, edst_v), (esrc_ref, esrc_v), (ew_ref, ew_v)))]
+    for copy in local:
+        copy.start()
+    project(0, x_ref[...])
+    pl.semaphore_wait(barrier, rep_n + row_n - 1)
+
+    def send_y(level):
+        forward(level, 0).start()
+        for o in range(1, row_n):
+            y_copy(level, o).start()
+
+    send_y(0)
+    for o in range(1, rep_n):
+        for copy in edge_copies(o):
+            copy.start()
+
+    rows_a = lax.broadcasted_iota(jnp.int32, (BS, 1), 0)
+    rows_b = lax.broadcasted_iota(jnp.int32, (LANES, 1), 0)
+    nt = (((1,), (1,)), ((), ()))
+
+    def build(q):
+        def section(j, carry):
+            s = j * rep_n + q
+            for k in range(0, slots, 2):
+                total = None
+                masks = []
+                for h in range(2):
+                    d_row = edst_v[q, j, pl.ds(k + h, 1), :]
+                    s_row = esrc_v[q, j, pl.ds(k + h, 1), :]
+                    w_row = ew_v[q, j, pl.ds(k + h, 1), :]
+                    a = jnp.where(rows_a == d_row, w_row, 0.0).astype(jnp.bfloat16)
+                    b = jnp.where(rows_b == s_row + h * HALF, 1.0, 0.0).astype(jnp.bfloat16)
+                    part = lax.dot_general(a, b, nt, preferred_element_type=jnp.float32)
+                    total = part if total is None else total + part
+                    masks.append(code_s[q, 0, j * slots + k + h] // 8)
+                tile = total.astype(jnp.bfloat16)
+                where_to = jnp.where(low, masks[0], masks[1])
+                for d in range(rows // BS):
+                    keep = jnp.where(where_to == d, 1.0, 0.0).astype(jnp.bfloat16)
+                    big[s, d * BS:(d + 1) * BS, k * BS:(k + 2) * BS] = tile * keep
+            return carry
+
+        lax.fori_loop(0, sections, section, 0)
+
+    def gathered(level, s, turn):
+        pick = pick0 if turn % 2 == 0 else pick1
+        pick[...] = ybuf[level, s]
+        q = lax.rem(s, rep_n)
+        j = s // rep_n
+        parts = []
+        for k in range(slots):
+            src = lax.rem(code_s[q, 0, j * slots + k], 8)
+            block = pick[lax.rem(src, per_half)]
+            keep = jnp.where(lane // HALF == src // per_half, 1.0, 0.0).astype(jnp.bfloat16)
+            parts.append(block * keep)
+        return jnp.dot(big[s], jnp.concatenate(parts, axis=0), preferred_element_type=jnp.float32)
+
+    def here(p, o):
+        return p * row_n + at_row(row_n - o)
+
+    order = [1, row_n - 1] + list(range(2, row_n - 1)) if row_n > 2 else list(range(1, row_n))
+
+    for copy in local:
+        copy.wait()
+    build(rep)
+    for o in range(1, row_n):
+        y_copy(0, o).wait_recv()
+        forward(0, o).start()
+
+    def from_peer(o, carry):
+        q = at_rep(rep_n - o)
+        for copy in edge_copies(o):
+            copy.wait_recv()
+        fetch = pltpu.make_async_copy(code_v.at[q], code_s.at[q], l_sem.at[4])
+        fetch.start()
+        fetch.wait()
+        build(q)
+        return carry
+
+    lax.fori_loop(1, rep_n, from_peer, 0)
+
+    state = x_ref[...]
+    for level in range(LAYERS):
+        if level > 0:
+            project(level, state)
+            send_y(level)
+        acc = gathered(level, pipe * row_n + row, 0)
+        forward(level, 0).wait_recv()
+        acc = acc + gathered(level, here(other, 0), 1)
+        for o in order:
+            if level > 0:
+                y_copy(level, o).wait_recv()
+                forward(level, o).start()
+            acc = acc + gathered(level, here(pipe, o), o + 1)
+        for o in order:
+            forward(level, o).wait_recv()
+            acc = acc + gathered(level, here(other, o), o)
+        top, bottom = acc[:half_rows], acc[half_rows:]
+        packed = jnp.where(low, top + pltpu.roll(top, HALF, 1), bottom + pltpu.roll(bottom, HALF, 1))
+        cbuf[level, rep] = packed.astype(jnp.bfloat16)
+
+        def c_copy(o):
+            mine = cbuf.at[level, rep]
+            return pltpu.make_async_remote_copy(mine, mine, c_send.at[level, o], c_recv.at[level, o],
+                                                device_id={"rep": at_rep(o)}, device_id_type=MESH)
+
+        for o in range(1, rep_n):
+            c_copy(o).start()
+        own = jnp.dot(state, wself_ref[level], preferred_element_type=jnp.float32)
+        for o in range(1, rep_n):
+            c_copy(o).wait_recv()
+        tops, bottoms = [], []
+        for r in range(0, rep_n, 2):
+            even = cbuf[level, r].astype(jnp.float32)
+            odd = cbuf[level, r + 1].astype(jnp.float32)
+            tops.append(jnp.where(low, even, pltpu.roll(odd, HALF, 1)))
+            bottoms.append(jnp.where(low, pltpu.roll(even, HALF, 1), odd))
+        summed = jnp.concatenate([jnp.concatenate(tops, axis=1), jnp.concatenate(bottoms, axis=1)], axis=0)
+        stat = jnp.mean(summed * summed, axis=-1, keepdims=True)
+        pre = own + summed * lax.rsqrt(stat + 1e-05) * gain_ref[pl.ds(level, 1), :]
+        first = (pre / (1.0 + jnp.exp(-pre))).astype(jnp.bfloat16)
+        mid = jnp.dot(first, wmid_ref[level], preferred_element_type=jnp.float32)
+        second = (mid / (1.0 + jnp.exp(-mid))).astype(jnp.bfloat16)
+        state = (state.astype(jnp.float32)
+                 + jnp.dot(second, wout_ref[level], preferred_element_type=jnp.float32)).astype(jnp.bfloat16)
+        out_ref[level, 0] = state
+        for o in range(1, rep_n):
+            c_copy(o).wait_send()
+        for o in range(1, row_n):
+            y_copy(level, o).wait_send()
+        for o in range(row_n):
+            forward(level, o).wait_send()
+    for o in range(1, rep_n):
+        for copy in edge_copies(o):
+            copy.wait_send()
+
+
+def fused(features, tile_src, tile_dst, tile_count, edge_dst, edge_src, edge_weight, w_msg, w_self, w_mid, w_out, gain):
+    _, rows, width = features.shape
+    sections, slots, edges = edge_dst.shape[2:]
+    rep_n, row_n, pipe_n = lax.axis_size("rep"), lax.axis_size("row"), lax.axis_size("pipe")
+    groups = row_n * pipe_n
+    live = jnp.arange(slots)[None, :] < tile_count[0, 0][:, None]
+    code = (tile_src[0, 0] + 8 * jnp.where(live, tile_dst[0, 0], 8)).reshape(1, sections * slots)
+    code = jnp.pad(code, ((0, 7), (0, LANES - sections * slots)))
+    vmem = pl.BlockSpec(memory_space=pltpu.VMEM)
+    dma = pltpu.SemaphoreType.DMA
+    return pl.pallas_call(
+        functools.partial(fused_body, (rows, width, slots, sections, rep_n, row_n)),
+        out_shape=jax.ShapeDtypeStruct((LAYERS, 1, rows, width), jnp.bfloat16),
+        in_specs=[vmem] * 10,
+        out_specs=vmem,
+        scratch_shapes=[
+            pltpu.VMEM((rep_n, 8, LANES), jnp.int32),
+            pltpu.SMEM((rep_n, 8, LANES), jnp.int32),
+            pltpu.VMEM((rep_n, sections, slots, edges), jnp.int32),
+            pltpu.VMEM((rep_n, sections, slots, edges), jnp.int32),
+            pltpu.VMEM((rep_n, sections, slots, edges), jnp.float32),
+            pltpu.VMEM((groups, rows, slots * BS), jnp.bfloat16),
+            pltpu.VMEM((LAYERS, groups, rows // BS // 2, BS, LANES), jnp.bfloat16),
+            pltpu.VMEM((LAYERS, rep_n, rows // 2, LANES), jnp.bfloat16),
+            pltpu.VMEM((rows // BS // 2, BS, LANES), jnp.bfloat16),
+            pltpu.VMEM((rows // BS // 2, BS, LANES), jnp.bfloat16),
+            dma((rep_n, 4)), dma((rep_n, 4)), dma((5,)),
+            dma((LAYERS, row_n)), dma((LAYERS, row_n)),
+            dma((LAYERS, row_n)), dma((LAYERS, row_n)),
+            dma((LAYERS, rep_n)), dma((LAYERS, rep_n)),
+        ],
+        compiler_params=pltpu.CompilerParams(
+            collective_id=0, has_side_effects=True, vmem_limit_bytes=40 * 1024 * 1024),
+    )(features[0], code, edge_dst[0, 0], edge_src[0, 0], edge_weight[0, 0], w_msg, w_self, w_mid, w_out, gain)
+
+
+def on_device(*args):
+    events, rows, width = args[0].shape
+    sections, slots = args[4].shape[2:4]
+    groups = lax.axis_size("row") * lax.axis_size("pipe")
+    rep_n = lax.axis_size("rep")
+    fits = (
+        events == 1
+        and lax.axis_size("pipe") == 2
+        and rows // BS == 8
+        and width == rep_n * HALF
+        and rep_n % 2 == 0
+        and sections * rep_n == groups
+        and slots % 2 == 0
+        and sections * slots <= LANES
+        and groups * rows * slots * BS * 2 <= 16 * 1024 * 1024
+    )
+    return fused(*args) if fits else by_sections(*args)
+
+
 def solution(mesh):
     placed = (
         P(None, ("pipe", "row"), None),

time: 141 us -> 50 us (0.35)
  blocking collectives: 100 us -> 0 us
  Pallas kernels: 0 us -> 40.4 us
  matrix products: 15.4 us -> 0 us
  local copies, waits for them, and re-layouts: 20.9 us -> 9.1 us
  other arithmetic: 2.33 us -> 0.08 us
  loops' own time: 1.8 us -> 0 us
    all_gather x6 -> x0, blocking collectives: 100 us -> none  [the longest x2 54.3 us: on_device(): piece = lax.all_gather(y_share, ('pipe', 'row'), axis=0, tiled=True)]
    pallas_call x0 -> x1, Pallas kernels: none -> 40.4 us  [fused(): pl.pallas_call(functools.partial(fused_body, (rows, width, slots, section...]
    dot_general x39 -> x0, matrix products: 15.4 us -> none  [the longest x16 6.06 us: section_product(): jnp.einsum('kn,kaf->naf', hot_now, prod, precision=lax.Precision.HIGHEST)]
    gather x16 -> x0, local copies, waits for them, and re-layouts: 9.42 us -> none  [section_product(): picked = jnp.take(blocked, src_now, axis=0)]
    unnamed x22 -> x24, local copies, waits for them, and re-layouts: 0.55 us -> 8.83 us
    dot_general x16 -> x0, local copies, waits for them, and re-layouts: 4.37 us -> none  [section_product(): jnp.einsum('kab,kbf->kaf', tiles_now, picked, preferred_element_type=jnp....]
    dynamic_slice x32 -> x0, local copies, waits for them, and re-layouts: 2.07 us -> none  [one_block(): sub = lax.dynamic_slice_in_dim(piece, i * rows, rows, 0)]
    reshape x16 -> x0, local copies, waits for them, and re-layouts: 1.86 us -> none  [section_product(): return summed.reshape(rows, width)]
where the time goes in v1:
time: 50 us; the launch traced here: 49.6 us
  Pallas kernels  40.4 us (81%)
  local copies, waits for them, and re-layouts  9.1 us (18%)
    pallas_call x1, Pallas kernels, fused(): pl.pallas_call(functools.partial(fused_body, (rows, width, slots, section...  40.4 us
    unnamed x24, local copies, waits for them, and re-layouts  8.83 us

profile of v1, /device:TPU:0, one launch (start us, length us, event | category | flops | bytes accessed | tf_op | source)
XLA Modules:
  0.0 49.6 jit_solution(2204168292260088619)
XLA Ops:
  0.0 0.0 copy-start.8
  0.0 0.7 %copy-done.8 = s32[1,1,2,12]{3,2,1,0:T(2,128)S(1)} copy-done((s32[1,1,2,12]{3,2,1,0:T(2,128)S(1)}, s32[1,1,2,12]{3,2,1,0:T(2,128)}, u32[]{:S(2)}) %copy-start.8) | copy-done | bytes 120
  0.7 0.0 copy-start.9
  0.7 0.1 squeeze.19
  0.8 0.6 %copy-done.9 = s32[1,1,2,12]{3,2,1,0:T(2,128)S(1)} copy-done((s32[1,1,2,12]{3,2,1,0:T(2,128)S(1)}, s32[1,1,2,12]{3,2,1,0:T(2,128)}, u32[]{:S(2)}) %copy-start.9) | copy-done | bytes 120
  1.4 0.0 copy-start.10
  1.4 0.1 squeeze.20
  1.4 0.6 %copy-done.10 = s32[1,1,2]{2,1,0:T(1,128)S(1)} copy-done((s32[1,1,2]{2,1,0:T(1,128)S(1)}, s32[1,1,2]{2,1,0:T(1,128)}, u32[]{:S(2)}) %copy-start.10) | copy-done | bytes 32
  2.0 0.1 iota_compare_fusion
  2.1 0.1 lt.29
  2.2 0.0 copy-start.6
  2.2 0.0 copy-start.7
  2.2 0.8 %copy.19 = f32[1,1,2,12,256]{4,3,2,1,0:T(8,128)S(1)} copy(f32[1,1,2,12,256]{4,2,3,1,0:T(2,128)} %param.18) | data formatting | bytes 49152 | tf_op args[6]
  3.0 0.0 copy-done.6
  3.0 0.0 copy-done.7
  3.0 0.0 copy-start.5
  3.0 0.7 %copy-done.5 = f32[2,256]{1,0:T(2,128)S(1)} copy-done((f32[2,256]{1,0:T(2,128)S(1)}, f32[2,256]{1,0:T(2,128)}, u32[]{:S(2)}) %copy-start.5) | copy-done | bytes 2072
  3.7 0.9 %copy-done = bf16[1,512,256]{2,1,0:T(8,128)(2,1)S(1)} copy-done((bf16[1,512,256]{2,1,0:T(8,128)(2,1)S(1)}, bf16[1,512,256]{2,1,0:T(8,128)(2,1)}, u32[]{:S(2)}) %copy-start) | copy-done | bytes 262168
  4.6 0.9 %copy-done.1 = bf16[2,256,256]{2,1,0:T(8,128)(2,1)S(1)} copy-done((bf16[2,256,256]{2,1,0:T(8,128)(2,1)S(1)}, bf16[2,256,256]{2,1,0:T(8,128)(2,1)}, u32[]{:S(2)}) %copy-start.1) | copy-done | bytes 262168
  5.6 0.9 %copy-done.2 = bf16[2,256,256]{2,1,0:T(8,128)(2,1)S(1)} copy-done((bf16[2,256,256]{2,1,0:T(8,128)(2,1)S(1)}, bf16[2,256,256]{2,1,0:T(8,128)(2,1)}, u32[]{:S(2)}) %copy-start.2) | copy-done | bytes 262168
  6.5 0.9 %copy-done.3 = bf16[2,256,256]{2,1,0:T(8,128)(2,1)S(1)} copy-done((bf16[2,256,256]{2,1,0:T(8,128)(2,1)S(1)}, bf16[2,256,256]{2,1,0:T(8,128)(2,1)}, u32[]{:S(2)}) %copy-start.3) | copy-done | bytes 262168
  7.5 0.9 %copy-done.4 = bf16[2,256,256]{2,1,0:T(8,128)(2,1)S(1)} copy-done((bf16[2,256,256]{2,1,0:T(8,128)(2,1)S(1)}, bf16[2,256,256]{2,1,0:T(8,128)(2,1)}, u32[]{:S(2)}) %copy-start.4) | copy-done | bytes 262168
  8.4 40.4 %shard_map.118 = bf16[2,1,512,256]{3,2,1,0:T(8,128)(2,1)S(1)} custom-call(bf16[512,256]{1,0:T(8,128)(2,1)S(1)} %bitcast.9, s32[8,128]{1,0:T(8,128)S(1)} %pad.4.code_ref, s32[2,12,256]{2,1,0:T(8,128)S(1)} %get-tuple-element.6.edst_ref, s32[2,12,256]{2,1,0:T(8,128)S(1)} %get-tuple-element.5.esrc_ref, f32[2,12,256]{2,1,0:T(8,128)S(1)} %bitcast.10, ...), custom_call_target="tpu_custom_call" | custom-call | tf_op jit(solution)/shard_map/pallas_call | solution.py:315
  48.8 0.8 %copy.21 = bf16[2,1,512,256]{3,2,1,0:T(8,128)(2,1)} copy(bf16[2,1,512,256]{3,2,1,0:T(8,128)(2,1)S(1)} %shard_map.118) | data formatting | bytes 1048576
  (8 shorter events, 0.0 us)
Async XLA Ops:
  0.0 0.7 %copy-start.8 = (s32[1,1,2,12]{3,2,1,0:T(2,128)S(1)}, s32[1,1,2,12]{3,2,1,0:T(2,128)}, u32[]{:S(2)}) copy-start(s32[1,1,2,12]{3,2,1,0:T(2,128)} %param.13) | copy-start | bytes 292
  0.7 0.7 %copy-start.9 = (s32[1,1,2,12]{3,2,1,0:T(2,128)S(1)}, s32[1,1,2,12]{3,2,1,0:T(2,128)}, u32[]{:S(2)}) copy-start(s32[1,1,2,12]{3,2,1,0:T(2,128)} %param.14) | copy-start | bytes 292
  1.4 0.7 %copy-start.10 = (s32[1,1,2]{2,1,0:T(1,128)S(1)}, s32[1,1,2]{2,1,0:T(1,128)}, u32[]{:S(2)}) copy-start(s32[1,1,2]{2,1,0:T(1,128)} %param.15) | copy-start | bytes 28
  2.2 0.8 %copy-start.6 = (s32[1,1,2,12,256]{4,2,3,1,0:T(2,128)S(1)}, s32[1,1,2,12,256]{4,2,3,1,0:T(2,128)}, u32[]{:S(2)}) copy-start(s32[1,1,2,12,256]{4,2,3,1,0:T(2,128)} %param.17) | copy-start | bytes 73732
  2.2 0.8 %copy-start.7 = (s32[1,1,2,12,256]{4,2,3,1,0:T(2,128)S(1)}, s32[1,1,2,12,256]{4,2,3,1,0:T(2,128)}, u32[]{:S(2)}) copy-start(s32[1,1,2,12,256]{4,2,3,1,0:T(2,128)} %param.16) | copy-start | bytes 73732
  3.0 0.7 %copy-start.5 = (f32[2,256]{1,0:T(2,128)S(1)}, f32[2,256]{1,0:T(2,128)}, u32[]{:S(2)}) copy-start(f32[2,256]{1,0:T(2,128)} %gain_ref.1) | copy-start | bytes 6148
  3.7 0.9 %copy-start = (bf16[1,512,256]{2,1,0:T(8,128)(2,1)S(1)}, bf16[1,512,256]{2,1,0:T(8,128)(2,1)}, u32[]{:S(2)}) copy-start(bf16[1,512,256]{2,1,0:T(8,128)(2,1)} %param.12) | copy-start | bytes 786436
  4.6 0.9 %copy-start.1 = (bf16[2,256,256]{2,1,0:T(8,128)(2,1)S(1)}, bf16[2,256,256]{2,1,0:T(8,128)(2,1)}, u32[]{:S(2)}) copy-start(bf16[2,256,256]{2,1,0:T(8,128)(2,1)} %wmsg_ref.1) | copy-start | bytes 786436
  5.6 0.9 %copy-start.2 = (bf16[2,256,256]{2,1,0:T(8,128)(2,1)S(1)}, bf16[2,256,256]{2,1,0:T(8,128)(2,1)}, u32[]{:S(2)}) copy-start(bf16[2,256,256]{2,1,0:T(8,128)(2,1)} %wself_ref.1) | copy-start | bytes 786436
  6.5 0.9 %copy-start.3 = (bf16[2,256,256]{2,1,0:T(8,128)(2,1)S(1)}, bf16[2,256,256]{2,1,0:T(8,128)(2,1)}, u32[]{:S(2)}) copy-start(bf16[2,256,256]{2,1,0:T(8,128)(2,1)} %wmid_ref.1) | copy-start | bytes 786436
  7.5 0.9 %copy-start.4 = (bf16[2,256,256]{2,1,0:T(8,128)(2,1)S(1)}, bf16[2,256,256]{2,1,0:T(8,128)(2,1)}, u32[]{:S(2)}) copy-start(bf16[2,256,256]{2,1,0:T(8,128)(2,1)} %wout_ref.1) | copy-start | bytes 786436
